TPU v7x, 256 devices: a whole 4x4x8 slice. The times are simulated.
256 devices in a mesh: tm: 8 (over x, core), row: 32 (over z, y).
Axes of the slice: x: 4, y: 4, z: 8, core: 2. Of those that a mesh axis runs over, the one named last changes fastest.
Arguments:
- pred_cov: bfloat16 [8, 1536, 1536], P('tm', 'row'), may hold values from -0.8 to 3.3, as said below
- cross: float32 [8, 1536, 1536], P('tm', 'row'), may hold values from -0.9 to 3.2
- filt_mean: float32 [8, 1536], P('tm', 'row'), may hold values from -6 to 6
- pred_mean: float32 [8, 1536], P('tm', 'row'), may hold values from -6 to 6
- next_smoothed: float32 [1536], P('row'), may hold values from -6 to 6
Outputs:
- smoothed: float32 [8, 1536], P('tm', 'row')
- gains: float32 [8, 1536, 1536], P('tm', 'row')
Inputs may be any that keep to these rules, and one draw needn't show every extreme that they name: `pred_cov`: each of the 8 matrices of size 1536 x 1536 is symmetric positive definite.
All inputs are finite; a program needn't handle non-finite values.
Results may differ from a plain program's by a relative error of at most 0.0003.
Values may be sent and summed in bfloat16 or wider, within the bound.
No kernel may reach another device: no remote copies, remote signals or barrier semaphores. Data moves between devices by JAX's collectives and lax.ppermute only.
A program may use at most 128 MiB of HBM per device.

v0:
```python
import jax
import jax.numpy as jnp
from jax import lax
from jax.sharding import PartitionSpec as P

finest = lax.Precision.HIGHEST


def from_behind(array, axis, by):
    peers = lax.axis_size(axis)
    pairs = [(i, i + by) for i in range(peers) if 0 <= i + by < peers]
    return lax.ppermute(array, axis, pairs)


def matvec(matrix, vector):
    return jnp.dot(matrix, vector, precision=finest, preferred_element_type=jnp.float32)


def per_device(pred_cov, cross, filt_mean, pred_mean, next_smoothed):
    whole_cov = lax.all_gather(pred_cov, "row", axis=1, tiled=True)
    cholesky_factor = jnp.linalg.cholesky(whole_cov[0].astype(jnp.float32))
    gain = jax.scipy.linalg.cho_solve((cholesky_factor, True), cross[0].T).T
    steps = lax.axis_size("tm")
    final = lax.axis_index("tm") == steps - 1
    mean_f = filt_mean[0]
    mean_p = pred_mean[0]

    def advance(turn, state):
        later = from_behind(state, "tm", -1)
        later = jnp.where(final, next_smoothed, later)
        dispersion = lax.all_gather(later - mean_p, "row", axis=0, tiled=True)
        return mean_f + matvec(gain, dispersion)

    smoothed = lax.fori_loop(0, steps, advance, jnp.zeros_like(mean_f))
    return (smoothed[None, :], gain[None, :, :])


def solution(mesh):
    in_specs = (
        P("tm", "row", None),
        P("tm", "row", None),
        P("tm", "row"),
        P("tm", "row"),
        P("row"),
    )
    out_specs = (P("tm", "row"), P("tm", "row", None))
    return jax.shard_map(
        per_device, mesh=mesh, in_specs=in_specs, out_specs=out_specs, check_vma=False
    )
```

profile of v0, /device:TPU:1, one launch (start us, length us, event | category | flops | bytes accessed | tf_op | source)
XLA Modules:
  0.0 1267.0 jit_solution(8773022271125293121)
XLA Ops:
  7.9 87.3 %all-gather.2.cloned.1.call-done = bf16[1,1536,1536]{2,1,0:T(8,128)(2,1)} async-done(((bf16[1,48,1536]{2,1,0:T(8,128)(2,1)}), bf16[1,1536,1536]{2,1,0:T(8,128)(2,1)}) %all-gather.2.cloned.1.call-update) | async-done | bytes 4718608 | tf_op jit(solution)/shard_map/all_gather | solution.py:20
  129.0 11.7 cholesky.341
  160.0 12.0 cholesky.362
  186.9 11.7 cholesky.385
  214.7 11.7 cholesky.715
  242.6 11.9 cholesky.734
  270.8 11.7 cholesky.754
  299.1 11.7 cholesky.774
  326.9 11.9 cholesky.794
  354.6 11.7 cholesky.814
  367.7 10.2 custom-call.106
  382.2 11.7 cholesky.834
  408.8 11.9 cholesky.854
  434.9 11.7 cholesky.872
  464.7 42.9 %while.12 = (s32[]{:T(128)}, f32[1536,1536]{1,0:T(8,128)}, s32[12,2]{0,1:T(2,128)S(1)}, f32[12,128,128]{2,1,0:T(8,128)}, s32[]{:T(128)}) while((s32[]{:T(128)}, f32[1536,1536]{1,0:T(8,128)}, s32[12,2]{0,1:T(2,128)S(1)}, f32[12,128,128]{2,1,0:T(8,128)}, s32[]{:T(128)}) %tuple.127), condition=%wide.while_cond, body=%wide.while_body.sunk | while | flops 2 | bytes 132705 | solution.py:22
  507.6 118.9 %custom-call.109 = f32[12,128,128]{1,2,0:T(8,128)S(1)} custom-call(f32[12,128,128]{2,1,0:T(8,128)} %get-tuple-element.47), custom_call_target="InvertDiagBlocksLowerTriangular" | custom-call | tf_op jit(solution)/shard_map/jit(_cho_solve)/triangular_solve | solution.py:22
  664.4 594.7 %while.13 = (s32[]{:T(128)}, f32[48]{0:T(128)S(1)}, pred[]{:T(512)}, f32[48]{0:T(128)S(1)}, f32[48]{0:T(128)S(1)}, /*index=5*/f32[48,1536]{1,0:T(8,128)S(1)}, f3...) while((s32[]{:T(128)}, f32[48]{0:T(128)S(1)}, ...), condition=%wide.region_25.26_spmd.clone, body=%wide.region_24.25_spmd.clone.sunk | while | flops 886470 | bytes 335592 | solution.py:34
  672.3 58.9 %all-reduce.4 = f32[1536]{0:T(1024)S(1)} all-reduce(f32[1536]{0:T(1024)S(1)} %fusion.208), channel_id=1, replica_groups=mesh['tm'=8,'row'=32] {'row'}, use_global_device_ids=true, to_apply=%add.1 | all-reduce | flops 1536 | bytes 12288 | tf_op jit(solution)/shard_map/while
  731.6 15.0 %collective-permute-start = (f32[48]{0:T(128)S(1)}, f32[48]{0:T(128)S(1)}, u32[]{:S(2)}, u32[]{:S(2)}) collective-permute-start(f32[48]{0:T(128)S(1)} %broadcast_select_fusion.3), channel_id=1, source_target_pairs={{32,0},{64,32},{96,64},{128,96},{160,128},{192,160},{224,192},{33,... | collective-permute-start | bytes 584 | tf_op jit(solution)/shard_map/while/body/eval_jaxpr/ppermute | solution.py:12
  749.3 56.8 %all-reduce.4 = f32[1536]{0:T(1024)S(1)} all-reduce(f32[1536]{0:T(1024)S(1)} %fusion.208), channel_id=1, replica_groups=mesh['tm'=8,'row'=32] {'row'}, use_global_device_ids=true, to_apply=%add.1 | all-reduce | flops 1536 | bytes 12288 | tf_op jit(solution)/shard_map/while
  806.5 14.3 %collective-permute-start = (f32[48]{0:T(128)S(1)}, f32[48]{0:T(128)S(1)}, u32[]{:S(2)}, u32[]{:S(2)}) collective-permute-start(f32[48]{0:T(128)S(1)} %broadcast_select_fusion.3), channel_id=1, source_target_pairs={{32,0},{64,32},{96,64},{128,96},{160,128},{192,160},{224,192},{33,... | collective-permute-start | bytes 584 | tf_op jit(solution)/shard_map/while/body/eval_jaxpr/ppermute | solution.py:12
  823.7 58.4 %all-reduce.4 = f32[1536]{0:T(1024)S(1)} all-reduce(f32[1536]{0:T(1024)S(1)} %fusion.208), channel_id=1, replica_groups=mesh['tm'=8,'row'=32] {'row'}, use_global_device_ids=true, to_apply=%add.1 | all-reduce | flops 1536 | bytes 12288 | tf_op jit(solution)/shard_map/while
  882.5 14.3 %collective-permute-start = (f32[48]{0:T(128)S(1)}, f32[48]{0:T(128)S(1)}, u32[]{:S(2)}, u32[]{:S(2)}) collective-permute-start(f32[48]{0:T(128)S(1)} %broadcast_select_fusion.3), channel_id=1, source_target_pairs={{32,0},{64,32},{96,64},{128,96},{160,128},{192,160},{224,192},{33,... | collective-permute-start | bytes 584 | tf_op jit(solution)/shard_map/while/body/eval_jaxpr/ppermute | solution.py:12
  900.2 57.0 %all-reduce.4 = f32[1536]{0:T(1024)S(1)} all-reduce(f32[1536]{0:T(1024)S(1)} %fusion.208), channel_id=1, replica_groups=mesh['tm'=8,'row'=32] {'row'}, use_global_device_ids=true, to_apply=%add.1 | all-reduce | flops 1536 | bytes 12288 | tf_op jit(solution)/shard_map/while
  957.6 13.5 %collective-permute-start = (f32[48]{0:T(128)S(1)}, f32[48]{0:T(128)S(1)}, u32[]{:S(2)}, u32[]{:S(2)}) collective-permute-start(f32[48]{0:T(128)S(1)} %broadcast_select_fusion.3), channel_id=1, source_target_pairs={{32,0},{64,32},{96,64},{128,96},{160,128},{192,160},{224,192},{33,... | collective-permute-start | bytes 584 | tf_op jit(solution)/shard_map/while/body/eval_jaxpr/ppermute | solution.py:12
  974.6 58.6 %all-reduce.4 = f32[1536]{0:T(1024)S(1)} all-reduce(f32[1536]{0:T(1024)S(1)} %fusion.208), channel_id=1, replica_groups=mesh['tm'=8,'row'=32] {'row'}, use_global_device_ids=true, to_apply=%add.1 | all-reduce | flops 1536 | bytes 12288 | tf_op jit(solution)/shard_map/while
  1033.6 13.5 %collective-permute-start = (f32[48]{0:T(128)S(1)}, f32[48]{0:T(128)S(1)}, u32[]{:S(2)}, u32[]{:S(2)}) collective-permute-start(f32[48]{0:T(128)S(1)} %broadcast_select_fusion.3), channel_id=1, source_target_pairs={{32,0},{64,32},{96,64},{128,96},{160,128},{192,160},{224,192},{33,... | collective-permute-start | bytes 584 | tf_op jit(solution)/shard_map/while/body/eval_jaxpr/ppermute | solution.py:12
  1051.1 56.7 %all-reduce.4 = f32[1536]{0:T(1024)S(1)} all-reduce(f32[1536]{0:T(1024)S(1)} %fusion.208), channel_id=1, replica_groups=mesh['tm'=8,'row'=32] {'row'}, use_global_device_ids=true, to_apply=%add.1 | all-reduce | flops 1536 | bytes 12288 | tf_op jit(solution)/shard_map/while
  1108.2 13.1 %collective-permute-start = (f32[48]{0:T(128)S(1)}, f32[48]{0:T(128)S(1)}, u32[]{:S(2)}, u32[]{:S(2)}) collective-permute-start(f32[48]{0:T(128)S(1)} %broadcast_select_fusion.3), channel_id=1, source_target_pairs={{32,0},{64,32},{96,64},{128,96},{160,128},{192,160},{224,192},{33,... | collective-permute-start | bytes 584 | tf_op jit(solution)/shard_map/while/body/eval_jaxpr/ppermute | solution.py:12
  1125.6 58.9 %all-reduce.4 = f32[1536]{0:T(1024)S(1)} all-reduce(f32[1536]{0:T(1024)S(1)} %fusion.208), channel_id=1, replica_groups=mesh['tm'=8,'row'=32] {'row'}, use_global_device_ids=true, to_apply=%add.1 | all-reduce | flops 1536 | bytes 12288 | tf_op jit(solution)/shard_map/while
  1184.8 12.6 collective-permute-start
  1202.0 56.7 %all-reduce.4 = f32[1536]{0:T(1024)S(1)} all-reduce(f32[1536]{0:T(1024)S(1)} %fusion.208), channel_id=1, replica_groups=mesh['tm'=8,'row'=32] {'row'}, use_global_device_ids=true, to_apply=%add.1 | all-reduce | flops 1536 | bytes 12288 | tf_op jit(solution)/shard_map/while
  (293 shorter events, 321.6 us)
Async XLA Ops:
  7.2 88.1 %all-gather.2.cloned.1.call-start = ((), (), s32[]{:S(2)}) async-start(), calls=%async_computation | async-start | bytes 4866048 | tf_op jit(solution)/shard_map/all_gather | solution.py:20
  125.3 3.6 copy-start
  456.2 170.3 %copy-start.2 = (f32[1,48,1536]{2,1,0:T(8,128)S(1)}, f32[1,48,1536]{2,1,0:T(8,128)}, u32[]{:S(2)}) copy-start(f32[1,48,1536]{2,1,0:T(8,128)} %param.8) | copy-start | bytes 884740
  630.6 33.7 %copy-start.3 = (f32[1,48]{1,0:T(1,128)S(1)}, f32[1,48]{1,0:T(1,128)}, u32[]{:S(2)}) copy-start(f32[1,48]{1,0:T(1,128)} %param.9) | copy-start | bytes 580
  630.6 33.7 %copy-start.4 = (f32[48]{0:T(128)S(1)}, f32[48]{0:T(128)}, u32[]{:S(2)}) copy-start(f32[48]{0:T(128)} %param.11) | copy-start | bytes 580
  630.6 33.7 %copy-start.5 = (f32[1,48]{1,0:T(1,128)S(1)}, f32[1,48]{1,0:T(1,128)}, u32[]{:S(2)}) copy-start(f32[1,48]{1,0:T(1,128)} %param.10) | copy-start | bytes 580
  630.7 33.7 %copy-start.6 = (u32[256]{0:T(256)S(1)}, u32[256]{0:T(256)}, u32[]{:S(2)}) copy-start(u32[256]{0:T(256)} %constant.815) | copy-start | bytes 3076
  664.4 7.9 collective-permute-start
  731.6 17.5 %collective-permute-start = (f32[48]{0:T(128)S(1)}, f32[48]{0:T(128)S(1)}, u32[]{:S(2)}, u32[]{:S(2)}) collective-permute-start(f32[48]{0:T(128)S(1)} %broadcast_select_fusion.3), channel_id=1, source_target_pairs={{32,0},{64,32},{96,64},{128,96},{160,128},{192,160},{224,192},{33,... | collective-permute-start | bytes 584 | tf_op jit(solution)/shard_map/while/body/eval_jaxpr/ppermute | solution.py:12
  806.5 17.2 %collective-permute-start = (f32[48]{0:T(128)S(1)}, f32[48]{0:T(128)S(1)}, u32[]{:S(2)}, u32[]{:S(2)}) collective-permute-start(f32[48]{0:T(128)S(1)} %broadcast_select_fusion.3), channel_id=1, source_target_pairs={{32,0},{64,32},{96,64},{128,96},{160,128},{192,160},{224,192},{33,... | collective-permute-start | bytes 584 | tf_op jit(solution)/shard_map/while/body/eval_jaxpr/ppermute | solution.py:12
  882.5 17.5 %collective-permute-start = (f32[48]{0:T(128)S(1)}, f32[48]{0:T(128)S(1)}, u32[]{:S(2)}, u32[]{:S(2)}) collective-permute-start(f32[48]{0:T(128)S(1)} %broadcast_select_fusion.3), channel_id=1, source_target_pairs={{32,0},{64,32},{96,64},{128,96},{160,128},{192,160},{224,192},{33,... | collective-permute-start | bytes 584 | tf_op jit(solution)/shard_map/while/body/eval_jaxpr/ppermute | solution.py:12
  957.6 16.9 %collective-permute-start = (f32[48]{0:T(128)S(1)}, f32[48]{0:T(128)S(1)}, u32[]{:S(2)}, u32[]{:S(2)}) collective-permute-start(f32[48]{0:T(128)S(1)} %broadcast_select_fusion.3), channel_id=1, source_target_pairs={{32,0},{64,32},{96,64},{128,96},{160,128},{192,160},{224,192},{33,... | collective-permute-start | bytes 584 | tf_op jit(solution)/shard_map/while/body/eval_jaxpr/ppermute | solution.py:12
  1033.6 17.4 %collective-permute-start = (f32[48]{0:T(128)S(1)}, f32[48]{0:T(128)S(1)}, u32[]{:S(2)}, u32[]{:S(2)}) collective-permute-start(f32[48]{0:T(128)S(1)} %broadcast_select_fusion.3), channel_id=1, source_target_pairs={{32,0},{64,32},{96,64},{128,96},{160,128},{192,160},{224,192},{33,... | collective-permute-start | bytes 584 | tf_op jit(solution)/shard_map/while/body/eval_jaxpr/ppermute | solution.py:12
  1108.2 17.3 %collective-permute-start = (f32[48]{0:T(128)S(1)}, f32[48]{0:T(128)S(1)}, u32[]{:S(2)}, u32[]{:S(2)}) collective-permute-start(f32[48]{0:T(128)S(1)} %broadcast_select_fusion.3), channel_id=1, source_target_pairs={{32,0},{64,32},{96,64},{128,96},{160,128},{192,160},{224,192},{33,... | collective-permute-start | bytes 584 | tf_op jit(solution)/shard_map/while/body/eval_jaxpr/ppermute | solution.py:12
  1184.8 17.1 %collective-permute-start = (f32[48]{0:T(128)S(1)}, f32[48]{0:T(128)S(1)}, u32[]{:S(2)}, u32[]{:S(2)}) collective-permute-start(f32[48]{0:T(128)S(1)} %broadcast_select_fusion.3), channel_id=1, source_target_pairs={{32,0},{64,32},{96,64},{128,96},{160,128},{192,160},{224,192},{33,... | collective-permute-start | bytes 584 | tf_op jit(solution)/shard_map/while/body/eval_jaxpr/ppermute | solution.py:12
  1259.0 0.7 copy-start.1
  1259.1 0.7 copy-start.7
Sparse Core Ops, SparseCore 0:
  10.6 84.6 all-gather.1
where the time goes:
time: 1290 us; the launch traced here: 1270 us
  blocking collectives  462 us (36%)
  other arithmetic  406 us (31%)
  waiting for transfers between devices  104 us (8%)
  starting transfers between devices  102 us (8%)
  matrix products  89.3 us (7%)
  local copies, waits for them, and re-layouts  74.1 us (6%)
  between operations  23.1 us (2%)
    while x8, blocking collectives  462 us
    another operation x46, other arithmetic, per_device(): cholesky_factor = jnp.linalg.cholesky(whole_cov[0].astype(jnp.float32))  264 us
    another operation x3, other arithmetic, per_device(): gain = jax.scipy.linalg.cho_solve((cholesky_factor, True), cross[0].T).T  127 us
    ppermute x8, starting transfers between devices, from_behind(): return lax.ppermute(array, axis, pairs)  102 us
    all_gather x1, waiting for transfers between devices, per_device(): whole_cov = lax.all_gather(pred_cov, 'row', axis=1, tiled=True)  87.3 us
    another operation x22, matrix products, per_device(): cholesky_factor = jnp.linalg.cholesky(whole_cov[0].astype(jnp.float32))  50.1 us
    another operation x36, local copies, waits for them, and re-layouts  42.9 us
    another operation x46, matrix products, per_device(): gain = jax.scipy.linalg.cho_solve((cholesky_factor, True), cross[0].T).T  36.7 us
  transfers between devices with their start and end apart: 9, of which 9 were waited for; matrix products, arithmetic and copies ran while one was open for 0% of the time, Pallas kernels for 0%

commit v1 on v0

v1 whole, which is shorter than its diff:
```python
import jax
import jax.numpy as jnp
from jax import lax
from jax.experimental import pallas as pl
from jax.experimental.pallas import tpu as pltpu
from jax.sharding import PartitionSpec as P

f32, bf16 = jnp.float32, jnp.bfloat16
N, B, H, LANES = 1536, 256, 128, 128
NB = N // B
VMEM_WHOLE = pl.BlockSpec(memory_space=pltpu.VMEM)

def inv4(d):
    a,b,c=d[0][0],d[1][0],d[1][1]
    r=1.0/(a*c-b*b)
    p,q,s=c*r,-b*r,a*r
    e0,e1,g0,g1=d[2][0],d[2][1],d[3][0],d[3][1]
    x00,x01=e0*p+e1*q,e0*q+e1*s
    x10,x11=g0*p+g1*q,g0*q+g1*s
    u=d[2][2]-(x00*e0+x01*e1)
    v=d[3][2]-(x10*e0+x11*e1)
    w=d[3][3]-(x10*g0+x11*g1)
    r2=1.0/(u*w-v*v)
    U,V,W=w*r2,-v*r2,u*r2
    y00,y01=U*x00+V*x10,U*x01+V*x11
    y10,y11=V*x00+W*x10,V*x01+W*x11
    i00=p+x00*y00+x10*y10
    i01=q+x00*y01+x10*y11
    i11=s+x01*y01+x11*y11
    return [[i00,i01,-y00,-y10],[i01,i11,-y01,-y11],[-y00,-y01,U,V],[-y10,-y11,V,W]]

def leaf(m_ref, K=4):
    n=m_ref.shape[0]
    lane=lax.broadcasted_iota(jnp.int32,(1,n),1)
    lanef=lax.broadcasted_iota(jnp.int32,(n,n),1)
    for p0 in range(0,n,K):
        M=m_ref[...]
        c=[jnp.broadcast_to(M[:,p0+q:p0+q+1],(n,n)) for q in range(K)]
        d=[[c[j][p0+i:p0+i+1,:] for j in range(i+1)] for i in range(K)]
        Di=inv4(d)
        r=[M[p0+q:p0+q+1,:] for q in range(K)]
        t=[]
        for i in range(K):
            x=Di[i][0]*r[0]
            for j in range(1,K): x=x+Di[i][j]*r[j]
            for j in range(K): x=jnp.where(lane==p0+j,-Di[i][j],x)
            t.append(x)
        new=jnp.where((lanef>=p0)&(lanef<p0+K),0.0,M)
        for q in range(K): new=new-c[q]*t[q]
        m_ref[...]=new
        m_ref[p0:p0+K,:]=jnp.concatenate(t,0)

def split(x):
    h=x.astype(bf16); return h,(x-h.astype(f32)).astype(bf16)

def dot3(a,b):
    ah,al=split(a); bh,bl=split(b)
    return jnp.dot(jnp.concatenate([ah,ah,al],1),jnp.concatenate([bh,bl,bh],0),preferred_element_type=f32)

def kern(p_ref,c_ref,w_ref,g_ref,m_ref,di_ref,t3_ref,c3_ref,cd_ref):
    w_ref[...]=p_ref[...].astype(f32)
    def step(k,_):
        o=pl.multiple_of(k*B,B)
        D=w_ref.at[pl.ds(o,B),pl.ds(o,B)]
        m_ref[...]=D[:H,:H]; leaf(m_ref); ai=-m_ref[...]
        b=D[:H,H:]; bt=D[H:,:H]
        X=dot3(ai,b); Xt=dot3(bt,ai)
        m_ref[...]=D[H:,H:]-dot3(bt,X)
        leaf(m_ref); si=-m_ref[...]
        XS=dot3(X,si)
        di_ref[:H,:H]=ai+dot3(XS,Xt)
        di_ref[:H,H:]=-XS
        di_ref[H:,:H]=-dot3(si,Xt)
        di_ref[H:,H:]=si
        di=di_ref[...]
        R=w_ref[pl.ds(o,B),:]
        T=dot3(di,R)
        h,l=split(T)
        t3_ref[:B,:]=h; t3_ref[B:2*B,:]=l; t3_ref[2*B:,:]=h
        C=w_ref[:,pl.ds(o,B)]
        h,l=split(C)
        c3_ref[:,:B]=h; c3_ref[:,B:2*B]=h; c3_ref[:,2*B:]=l
        dh,dl=split(di)
        d3=jnp.concatenate([dh,dl,dh],0)
        def cdl(i,_):
            q=pl.multiple_of(i*B,B)
            cd_ref[pl.ds(q,B),:]=jnp.dot(c3_ref[pl.ds(q,B),:],d3,preferred_element_type=f32)
            return 0
        lax.fori_loop(0,NB,cdl,0)
        def upd(i,_):
            q=pl.multiple_of(i*B,B)
            w_ref[pl.ds(q,B),:]=w_ref[pl.ds(q,B),:]-jnp.dot(c3_ref[pl.ds(q,B),:],t3_ref[...],preferred_element_type=f32)
            return 0
        lax.fori_loop(0,NB,upd,0)
        w_ref[pl.ds(o,B),:]=T
        w_ref[:,pl.ds(o,B)]=cd_ref[...]
        w_ref[pl.ds(o,B),pl.ds(o,B)]=-di
        return 0
    lax.fori_loop(0,NB,step,0)
    c=c_ref[...]
    ch,cl=split(c)
    c3=jnp.concatenate([ch,ch,cl],1)
    def gains(j,_):
        q=pl.multiple_of(j*B,B)
        wh,wl=split(w_ref[:,pl.ds(q,B)])
        g_ref[:,pl.ds(q,B)]=-jnp.dot(c3,jnp.concatenate([wh,wl,wh],0),preferred_element_type=f32)
        return 0
    lax.fori_loop(0,NB,gains,0)

def inverse(p,c):
    return pl.pallas_call(kern,out_shape=[jax.ShapeDtypeStruct((N,N),f32),jax.ShapeDtypeStruct(c.shape,f32)],
      in_specs=[pl.BlockSpec(memory_space=pltpu.VMEM)]*2,out_specs=[pl.BlockSpec(memory_space=pltpu.VMEM)]*2,
      scratch_shapes=[pltpu.VMEM((H,H),f32),pltpu.VMEM((B,B),f32),pltpu.VMEM((3*B,N),bf16),pltpu.VMEM((N,3*B),bf16),pltpu.VMEM((N,B),f32)],
      compiler_params=pltpu.CompilerParams(vmem_limit_bytes=26<<20))(p,c)

def vectors_kernel(x_ref, o_ref):
    for j in range(N // LANES):
        rows = slice(j * LANES, (j + 1) * LANES)
        o_ref[:, rows] = x_ref[rows, :].T[:8, :]


def vectors(packed):
    return pl.pallas_call(
        vectors_kernel,
        out_shape=jax.ShapeDtypeStruct((8, N), f32),
        grid=(1,),
        in_specs=[pl.BlockSpec((N, LANES), lambda i: (0, N // LANES))],
        out_specs=pl.BlockSpec((8, N), lambda i: (0, 0)),
        compiler_params=pltpu.CompilerParams(vmem_limit_bytes=4 << 20),
    )(packed)


def matvec(m_ref, v, out_ref):
    for i in range(N // LANES):
        rows = slice(i * LANES, (i + 1) * LANES)
        total = m_ref[rows, :LANES] * v[:, :LANES]
        for j in range(1, N // LANES):
            lanes = slice(j * LANES, (j + 1) * LANES)
            total = total + m_ref[rows, lanes] * v[:, lanes]
        out_ref[:, rows] = jnp.sum(total.T, axis=0, keepdims=True)


def turn_kernel(late_ref, base_ref, mean_ref, w_ref, c_ref, s_ref, y_ref):
    matvec(w_ref, late_ref[...] + base_ref[...], y_ref)
    matvec(c_ref, y_ref[...], s_ref)
    s_ref[...] = mean_ref[...] - s_ref[...]


def turn(late, base, mean, minus_inverse, packed):
    return pl.pallas_call(
        turn_kernel,
        out_shape=jax.ShapeDtypeStruct((1, N), f32),
        in_specs=[VMEM_WHOLE] * 5,
        out_specs=VMEM_WHOLE,
        scratch_shapes=[pltpu.VMEM((1, N), f32)],
        compiler_params=pltpu.CompilerParams(vmem_limit_bytes=4 << 20),
        cost_estimate=pl.CostEstimate(flops=4 * N * N, bytes_accessed=8 * N * N, transcendentals=0),
    )(late, base, mean, minus_inverse, packed)


def per_device(pred_cov, cross, filt_mean, pred_mean, next_smoothed):
    steps = lax.axis_size("tm")
    row = lax.axis_index("row")
    mine = cross.shape[1]
    whole_cov = lax.all_gather(pred_cov[0], "row", axis=0, tiled=True)
    columns = jnp.stack([filt_mean[0], pred_mean[0], next_smoothed], axis=1)
    packed = jnp.concatenate([cross[0], jnp.pad(columns, ((0, 0), (0, LANES - 3)))], axis=1)
    packed = lax.all_gather(packed, "row", axis=0, tiled=True)
    minus_inverse, gain = inverse(whole_cov, cross[0])
    rows = vectors(packed)
    mean = rows[0:1]
    final = lax.axis_index("tm") == steps - 1
    base = jnp.where(final, rows[2:3], 0.0) - rows[1:2]
    state = turn(jnp.zeros_like(mean), base, mean, minus_inverse, packed)
    for _ in range(steps - 1):
        late = lax.ppermute(state, "tm", [(i, i - 1) for i in range(1, steps)])
        state = turn(late, base, mean, minus_inverse, packed)
    smoothed = lax.dynamic_slice(state[0], (row * mine,), (mine,))
    return (smoothed[None, :], gain[None, :, :])


def solution(mesh):
    in_specs = (
        P("tm", "row", None),
        P("tm", "row", None),
        P("tm", "row"),
        P("tm", "row"),
        P("row"),
    )
    out_specs = (P("tm", "row"), P("tm", "row", None))
    return jax.shard_map(
        per_device, mesh=mesh, in_specs=in_specs, out_specs=out_specs, check_vma=False
    )
```

time: 1290 us -> 302 us (0.23); the launches traced: 1270 us -> 301 us
  blocking collectives: 462 us -> 0 us
  other arithmetic: 406 us -> 2.42 us
  Pallas kernels: 0 us -> 135 us
  matrix products: 89.3 us -> 0 us
  starting transfers between devices: 102 us -> 17.3 us
  local copies, waits for them, and re-layouts: 74.1 us -> 26.4 us
    while x8 -> x0, blocking collectives: 462 us -> none
    another operation x49 -> x1, other arithmetic: 392 us -> 0.7 us  [per_device(): columns = jnp.stack([filt_mean[0], pred_mean[0], next_smoothed], axis=1)]
    pallas_call x0 -> x10, Pallas kernels: none -> 135 us  [the longest x1 124 us: inverse(): pl.pallas_call(kern, out_shape=[jax.ShapeDtypeStruct((N, N), f32), jax.Sh...]
    another operation x68 -> x0, matrix products: 86.8 us -> none  [the longest x22 50.1 us: per_device(): cholesky_factor = jnp.linalg.cholesky(whole_cov[0].astype(jnp.float32))]
    ppermute x8 -> x7, starting transfers between devices: 102 us -> 17.2 us  [per_device(): late = lax.ppermute(state, 'tm', [(i, i - 1) for i in range(1, steps)])]
    another operation x57 -> x1, local copies, waits for them, and re-layouts: 47.9 us -> 0.09 us  [per_device(): columns = jnp.stack([filt_mean[0], pred_mean[0], next_smoothed], axis=1)]
    unnamed x68 -> x16, local copies, waits for them, and re-layouts: 4.62 us -> 25.7 us
    all_gather x1 -> x2, waiting for transfers between devices: 87.3 us -> 84.8 us  [the longest x1 84.8 us: per_device(): whole_cov = lax.all_gather(pred_cov[0], 'row', axis=0, tiled=True)]
  transfers between devices with their start and end apart: 9 -> 9, of which waited for: 9 -> 8; matrix products, arithmetic and copies ran while one was open for 0% -> 1% of each run, Pallas kernels for 0% -> 41%
where the time goes in v1:
time: 302 us; the launch traced here: 301 us
  Pallas kernels  135 us (45%)
  waiting for transfers between devices  106 us (35%)
  local copies, waits for them, and re-layouts  26.4 us (9%)
  starting transfers between devices  17.3 us (6%)
  between operations  14.1 us (5%)
    pallas_call x1, Pallas kernels, inverse(): pl.pallas_call(kern, out_shape=[jax.ShapeDtypeStruct((N, N), f32), jax.Sh...  124 us
    all_gather x1, waiting for transfers between devices, per_device(): whole_cov = lax.all_gather(pred_cov[0], 'row', axis=0, tiled=True)  84.8 us
    unnamed x16, local copies, waits for them, and re-layouts  25.7 us
    ppermute x7, waiting for transfers between devices, per_device(): late = lax.ppermute(state, 'tm', [(i, i - 1) for i in range(1, steps)])  20.3 us
    ppermute x7, starting transfers between devices, per_device(): late = lax.ppermute(state, 'tm', [(i, i - 1) for i in range(1, steps)])  17.2 us
    pallas_call x8, Pallas kernels, turn(): pl.pallas_call(turn_kernel, out_shape=jax.ShapeDtypeStruct((1, N), f32),...  10.5 us
  transfers between devices with their start and end apart: 9, of which 8 were waited for; matrix products, arithmetic and copies ran while one was open for 1% of the time, Pallas kernels for 41%

profile of v1, /device:TPU:1, one launch (start us, length us, event | category | flops | bytes accessed | tf_op | source)
XLA Modules:
  0.0 301.0 jit_solution(6751738957397569810)
XLA Ops:
  8.7 1.7 select_maximum_fusion
  10.5 84.8 %all-gather.6.cloned.1.call-done = bf16[1,1536,1536]{2,1,0:T(8,128)(2,1)} async-done(((bf16[1,48,1536]{2,1,0:T(8,128)(2,1)}), bf16[1,1536,1536]{2,1,0:T(8,128)(2,1)}) %all-gather.6.cloned.1.call-update) | async-done | bytes 4718608 | tf_op jit(solution)/shard_map/all_gather | solution.py:165
  95.2 2.3 copy-done.6
  98.5 124.2 %shard_map.69 = (f32[1536,1536]{1,0:T(8,128)S(1)}, f32[48,1536]{1,0:T(8,128)}) custom-call(bf16[1536,1536]{1,0:T(8,128)(2,1)S(1)} %bitcast.6, f32[48,1536]{1,0:T(8,128)S(1)} %bitcast.8), custom_call_target="tpu_custom_call" | custom-call | tf_op jit(solution)/shard_map/pallas_call | solution.py:111
  222.7 3.6 %copy-done.3 = f32[1536,1536]{1,0:T(8,128)} copy-done((f32[1536,1536]{1,0:T(8,128)}, f32[1536,1536]{1,0:T(8,128)S(1)}, u32[]{:S(2)}) %copy-start.3) | copy-done | bytes 9437208
  226.3 3.9 %copy-done = f32[1536,1664]{1,0:T(8,128)S(1)} copy-done((f32[1536,1664]{1,0:T(8,128)S(1)}, f32[1536,1664]{1,0:T(8,128)}, u32[]{:S(2)}) %copy-start) | copy-done | bytes 10223640
  230.5 3.6 %copy-done.1 = f32[1536,1664]{1,0:T(8,128)S(1)} copy-done((f32[1536,1664]{1,0:T(8,128)S(1)}, f32[1536,1664]{1,0:T(8,128)}, u32[]{:S(2)}) %copy-start.1) | copy-done | bytes 10223640
  234.1 3.7 %copy-done.4 = f32[1536,1536]{1,0:T(8,128)S(1)} copy-done((f32[1536,1536]{1,0:T(8,128)S(1)}, f32[1536,1536]{1,0:T(8,128)}, u32[]{:S(2)}) %copy-start.4) | copy-done | bytes 9437208
  237.8 1.3 shard_map.70
  239.1 5.7 %collective-permute-start = (f32[1,1536]{1,0:T(1,128)S(1)}, f32[1,1536]{1,0:T(1,128)S(1)}, u32[]{:S(2)}, u32[]{:S(2)}) collective-permute-start(f32[1,1536]{1,0:T(1,128)S(1)} %shard_map.70), channel_id=1, source_target_pairs={{32,0},{64,32},{96,64},{128,96},{160,128},{192,160},{224,192},{33,... | collective-permute-start | bytes 18440 | tf_op jit(solution)/shard_map/ppermute | solution.py:176
  244.9 2.2 collective-permute-done.late_ref
  247.1 1.3 shard_map.71
  248.4 1.9 collective-permute-start.1
  250.3 3.0 %collective-permute-done.1.late_ref = f32[1,1536]{1,0:T(1,128)S(1)} collective-permute-done((f32[1,1536]{1,0:T(1,128)S(1)}, f32[1,1536]{1,0:T(1,128)S(1)}, u32[]{:S(2)}, u32[]{:S(2)}) %collective-permute-start.1) | collective-permute-done | bytes 6176 | tf_op jit(solution)/shard_map/ppermute | solution.py:176
  253.3 1.3 shard_map.72
  254.7 1.9 collective-permute-start.2
  256.6 3.0 %collective-permute-done.2.late_ref = f32[1,1536]{1,0:T(1,128)S(1)} collective-permute-done((f32[1,1536]{1,0:T(1,128)S(1)}, f32[1,1536]{1,0:T(1,128)S(1)}, u32[]{:S(2)}, u32[]{:S(2)}) %collective-permute-start.2) | collective-permute-done | bytes 6176 | tf_op jit(solution)/shard_map/ppermute | solution.py:176
  259.6 1.3 shard_map.73
  260.9 1.9 collective-permute-start.3
  262.8 3.0 %collective-permute-done.3.late_ref = f32[1,1536]{1,0:T(1,128)S(1)} collective-permute-done((f32[1,1536]{1,0:T(1,128)S(1)}, f32[1,1536]{1,0:T(1,128)S(1)}, u32[]{:S(2)}, u32[]{:S(2)}) %collective-permute-start.3) | collective-permute-done | bytes 6176 | tf_op jit(solution)/shard_map/ppermute | solution.py:176
  265.9 1.3 shard_map.74
  267.2 1.9 collective-permute-start.4
  269.1 3.0 %collective-permute-done.4.late_ref = f32[1,1536]{1,0:T(1,128)S(1)} collective-permute-done((f32[1,1536]{1,0:T(1,128)S(1)}, f32[1,1536]{1,0:T(1,128)S(1)}, u32[]{:S(2)}, u32[]{:S(2)}) %collective-permute-start.4) | collective-permute-done | bytes 6176 | tf_op jit(solution)/shard_map/ppermute | solution.py:176
  272.1 1.3 shard_map.75
  273.4 1.9 collective-permute-start.5
  275.4 3.0 %collective-permute-done.5.late_ref = f32[1,1536]{1,0:T(1,128)S(1)} collective-permute-done((f32[1,1536]{1,0:T(1,128)S(1)}, f32[1,1536]{1,0:T(1,128)S(1)}, u32[]{:S(2)}, u32[]{:S(2)}) %collective-permute-start.5) | collective-permute-done | bytes 6176 | tf_op jit(solution)/shard_map/ppermute | solution.py:176
  278.4 1.3 shard_map.76
  279.7 1.9 collective-permute-start.6
  281.6 3.0 %collective-permute-done.6.late_ref = f32[1,1536]{1,0:T(1,128)S(1)} collective-permute-done((f32[1,1536]{1,0:T(1,128)S(1)}, f32[1,1536]{1,0:T(1,128)S(1)}, u32[]{:S(2)}, u32[]{:S(2)}) %collective-permute-start.6) | collective-permute-done | bytes 6176 | tf_op jit(solution)/shard_map/ppermute | solution.py:176
  284.6 3.9 %copy-done.2 = f32[1536,1664]{1,0:T(8,128)S(1)} copy-done((f32[1536,1664]{1,0:T(8,128)S(1)}, f32[1536,1664]{1,0:T(8,128)}, u32[]{:S(2)}) %copy-start.2) | copy-done | bytes 10223640
  288.5 3.7 %copy-done.5 = f32[1536,1536]{1,0:T(8,128)S(1)} copy-done((f32[1536,1536]{1,0:T(8,128)S(1)}, f32[1536,1536]{1,0:T(8,128)}, u32[]{:S(2)}) %copy-start.5) | copy-done | bytes 9437208
  292.2 1.3 shard_map.77
  (20 shorter events, 3.4 us)
Async XLA Ops:
  7.2 88.1 %all-gather.6.cloned.1.call-start = ((), (), s32[]{:S(2)}) async-start(), calls=%async_computation.1 | async-start | bytes 4866048 | tf_op jit(solution)/shard_map/all_gather | solution.py:165
  7.9 218.4 %all-gather.4.cloned.1.call-start = ((), (), s32[]{:S(2)}) async-start(), calls=%async_computation | async-start | bytes 10543104 | tf_op jit(solution)/shard_map/all_gather | solution.py:168
  95.2 2.3 copy-start.6
  97.6 1.0 copy-start.7
  222.7 3.6 %copy-start.3 = (f32[1536,1536]{1,0:T(8,128)}, f32[1536,1536]{1,0:T(8,128)S(1)}, u32[]{:S(2)}) copy-start(f32[1536,1536]{1,0:T(8,128)S(1)} %get-tuple-element.4.w_ref) | copy-start | bytes 28311556
  226.3 3.9 %copy-start = (f32[1536,1664]{1,0:T(8,128)S(1)}, f32[1536,1664]{1,0:T(8,128)}, u32[]{:S(2)}) copy-start(f32[1536,1664]{1,0:T(8,128)} %all-gather.4.cloned.1.call-done.x_ref.c_ref) | copy-start | bytes 30670852
  230.2 3.9 %copy-start.1 = (f32[1536,1664]{1,0:T(8,128)S(1)}, f32[1536,1664]{1,0:T(8,128)}, u32[]{:S(2)}) copy-start(f32[1536,1664]{1,0:T(8,128)} %all-gather.4.cloned.1.call-done.x_ref.c_ref) | copy-start | bytes 30670852
  234.1 3.7 %copy-start.4 = (f32[1536,1536]{1,0:T(8,128)S(1)}, f32[1536,1536]{1,0:T(8,128)}, u32[]{:S(2)}) copy-start(f32[1536,1536]{1,0:T(8,128)} %copy-done.3) | copy-start | bytes 28311556
  239.1 7.9 %collective-permute-start = (f32[1,1536]{1,0:T(1,128)S(1)}, f32[1,1536]{1,0:T(1,128)S(1)}, u32[]{:S(2)}, u32[]{:S(2)}) collective-permute-start(f32[1,1536]{1,0:T(1,128)S(1)} %shard_map.70), channel_id=1, source_target_pairs={{32,0},{64,32},{96,64},{128,96},{160,128},{192,160},{224,192},{33,... | collective-permute-start | bytes 18440 | tf_op jit(solution)/shard_map/ppermute | solution.py:176
  248.4 4.9 %collective-permute-start.1 = (f32[1,1536]{1,0:T(1,128)S(1)}, f32[1,1536]{1,0:T(1,128)S(1)}, u32[]{:S(2)}, u32[]{:S(2)}) collective-permute-start(f32[1,1536]{1,0:T(1,128)S(1)} %shard_map.71), channel_id=1, source_target_pairs={{32,0},{64,32},{96,64},{128,96},{160,128},{192,160},{224,192},{33,... | collective-permute-start | bytes 18440 | tf_op jit(solution)/shard_map/ppermute | solution.py:176
  254.7 4.9 %collective-permute-start.2 = (f32[1,1536]{1,0:T(1,128)S(1)}, f32[1,1536]{1,0:T(1,128)S(1)}, u32[]{:S(2)}, u32[]{:S(2)}) collective-permute-start(f32[1,1536]{1,0:T(1,128)S(1)} %shard_map.72), channel_id=1, source_target_pairs={{32,0},{64,32},{96,64},{128,96},{160,128},{192,160},{224,192},{33,... | collective-permute-start | bytes 18440 | tf_op jit(solution)/shard_map/ppermute | solution.py:176
  260.9 4.9 %collective-permute-start.3 = (f32[1,1536]{1,0:T(1,128)S(1)}, f32[1,1536]{1,0:T(1,128)S(1)}, u32[]{:S(2)}, u32[]{:S(2)}) collective-permute-start(f32[1,1536]{1,0:T(1,128)S(1)} %shard_map.73), channel_id=1, source_target_pairs={{32,0},{64,32},{96,64},{128,96},{160,128},{192,160},{224,192},{33,... | collective-permute-start | bytes 18440 | tf_op jit(solution)/shard_map/ppermute | solution.py:176
  267.2 4.9 %collective-permute-start.4 = (f32[1,1536]{1,0:T(1,128)S(1)}, f32[1,1536]{1,0:T(1,128)S(1)}, u32[]{:S(2)}, u32[]{:S(2)}) collective-permute-start(f32[1,1536]{1,0:T(1,128)S(1)} %shard_map.74), channel_id=1, source_target_pairs={{32,0},{64,32},{96,64},{128,96},{160,128},{192,160},{224,192},{33,... | collective-permute-start | bytes 18440 | tf_op jit(solution)/shard_map/ppermute | solution.py:176
  273.4 4.9 %collective-permute-start.5 = (f32[1,1536]{1,0:T(1,128)S(1)}, f32[1,1536]{1,0:T(1,128)S(1)}, u32[]{:S(2)}, u32[]{:S(2)}) collective-permute-start(f32[1,1536]{1,0:T(1,128)S(1)} %shard_map.75), channel_id=1, source_target_pairs={{32,0},{64,32},{96,64},{128,96},{160,128},{192,160},{224,192},{33,... | collective-permute-start | bytes 18440 | tf_op jit(solution)/shard_map/ppermute | solution.py:176
  279.7 4.9 %collective-permute-start.6 = (f32[1,1536]{1,0:T(1,128)S(1)}, f32[1,1536]{1,0:T(1,128)S(1)}, u32[]{:S(2)}, u32[]{:S(2)}) collective-permute-start(f32[1,1536]{1,0:T(1,128)S(1)} %shard_map.76), channel_id=1, source_target_pairs={{32,0},{64,32},{96,64},{128,96},{160,128},{192,160},{224,192},{33,... | collective-permute-start | bytes 18440 | tf_op jit(solution)/shard_map/ppermute | solution.py:176
  284.6 3.9 %copy-start.2 = (f32[1536,1664]{1,0:T(8,128)S(1)}, f32[1536,1664]{1,0:T(8,128)}, u32[]{:S(2)}) copy-start(f32[1536,1664]{1,0:T(8,128)} %all-gather.4.cloned.1.call-done.x_ref.c_ref) | copy-start | bytes 30670852
  288.5 3.7 %copy-start.5 = (f32[1536,1536]{1,0:T(8,128)S(1)}, f32[1536,1536]{1,0:T(8,128)}, u32[]{:S(2)}) copy-start(f32[1536,1536]{1,0:T(8,128)} %copy-done.3) | copy-start | bytes 28311556
Sparse Core Ops, SparseCore 0:
  10.6 84.6 all-gather.5
  97.8 107.2 all-gather.3

commit v2 on v1

v2 whole, which is shorter than its diff:
```python
import functools

import jax
import jax.numpy as jnp
from jax import lax
from jax.experimental import pallas as pl
from jax.experimental.pallas import tpu as pltpu
from jax.sharding import PartitionSpec as P

f32, bf16 = jnp.float32, jnp.bfloat16
N, LANES = 1536, 128
MINE = 48
PIECE = 4 * MINE
B = 2 * PIECE
H = 128
TILE = 512
Y, Z = 4, 8
VMEM_WHOLE = pl.BlockSpec(memory_space=pltpu.VMEM)
SMEM_WHOLE = pl.BlockSpec(memory_space=pltpu.SMEM)

def inv4(d):
    a,b,c=d[0][0],d[1][0],d[1][1]
    r=1.0/(a*c-b*b)
    p,q,s=c*r,-b*r,a*r
    e0,e1,g0,g1=d[2][0],d[2][1],d[3][0],d[3][1]
    x00,x01=e0*p+e1*q,e0*q+e1*s
    x10,x11=g0*p+g1*q,g0*q+g1*s
    u=d[2][2]-(x00*e0+x01*e1)
    v=d[3][2]-(x10*e0+x11*e1)
    w=d[3][3]-(x10*g0+x11*g1)
    r2=1.0/(u*w-v*v)
    U,V,W=w*r2,-v*r2,u*r2
    y00,y01=U*x00+V*x10,U*x01+V*x11
    y10,y11=V*x00+W*x10,V*x01+W*x11
    i00=p+x00*y00+x10*y10
    i01=q+x00*y01+x10*y11
    i11=s+x01*y01+x11*y11
    return [[i00,i01,-y00,-y10],[i01,i11,-y01,-y11],[-y00,-y01,U,V],[-y10,-y11,V,W]]

def leaf(m_ref, K=4):
    n=m_ref.shape[0]
    lane=lax.broadcasted_iota(jnp.int32,(1,n),1)
    lanef=lax.broadcasted_iota(jnp.int32,(n,n),1)
    for p0 in range(0,n,K):
        M=m_ref[...]
        c=[jnp.broadcast_to(M[:,p0+q:p0+q+1],(n,n)) for q in range(K)]
        d=[[c[j][p0+i:p0+i+1,:] for j in range(i+1)] for i in range(K)]
        Di=inv4(d)
        r=[M[p0+q:p0+q+1,:] for q in range(K)]
        t=[]
        for i in range(K):
            x=Di[i][0]*r[0]
            for j in range(1,K): x=x+Di[i][j]*r[j]
            for j in range(K): x=jnp.where(lane==p0+j,-Di[i][j],x)
            t.append(x)
        new=jnp.where((lanef>=p0)&(lanef<p0+K),0.0,M)
        for q in range(K): new=new-c[q]*t[q]
        m_ref[...]=new
        m_ref[p0:p0+K,:]=jnp.concatenate(t,0)


def split(x):
    h = x.astype(bf16)
    return h, (x - h.astype(f32)).astype(bf16)


def wide(x):
    h, l = split(x)
    return jnp.concatenate([h, h, l], 1)


def tall(x):
    h, l = split(x)
    return jnp.concatenate([h, l, h], 0)


def dot(a, b):
    return jnp.dot(a, b, preferred_element_type=f32)


def block_sweep(d_ref, m_ref, r_ref):
    def step(k, _):
        o = pl.multiple_of(k * H, H)
        m_ref[...] = d_ref[pl.ds(o, H), pl.ds(o, H)]
        leaf(m_ref)
        minus = m_ref[...]
        t = -dot(wide(minus), tall(d_ref[pl.ds(o, H), :]))
        c = wide(d_ref[:, pl.ds(o, H)])
        r_ref[...] = -dot(c, tall(minus))
        d_ref[...] = d_ref[...] - dot(c, tall(t))
        d_ref[pl.ds(o, H), :] = t
        d_ref[:, pl.ds(o, H)] = r_ref[...]
        d_ref[pl.ds(o, H), pl.ds(o, H)] = minus
        return 0

    lax.fori_loop(0, B // H, step, 0)


def stage_kernel(stage, ids, near_ref, far_ref, *refs):
    if stage:
        _, *refs = refs
    if stage == N // B - 1:
        cross_ref, *refs = refs
        w_ref, g_ref, p_ref, t3_ref, d_ref, m_ref, r_ref = refs
    else:
        w_ref, p_ref, t3_ref, d_ref, m_ref, r_ref = refs
    here = pl.multiple_of(ids[stage] * B, B)
    for n, ref in enumerate((near_ref, far_ref)):
        z = ids[4 + n]
        for d in range(Y):
            y = lax.rem(ids[6] + d, Y)
            to = pl.multiple_of(lax.rem(z, 2) * PIECE + y * MINE, 16)
            p_ref[pl.ds(to, MINE), :] = ref[d * MINE : (d + 1) * MINE, :]
    rows = pl.ds(here, B)
    w_ref[rows, :] = p_ref[...].astype(f32)
    if stage:

        def clear(j, _):
            w_ref[rows, pl.ds(pl.multiple_of(ids[j] * B, B), B)] = jnp.zeros((B, B), f32)
            return 0

        lax.fori_loop(0, stage, clear, 0)

        def earlier(j, _):
            there = pl.multiple_of(ids[j] * B, B)
            p = p_ref[:, pl.ds(there, B)]
            p = jnp.concatenate([p, p], 1)

            def tile(n, _):
                q = pl.ds(pl.multiple_of(n * TILE, TILE), TILE)
                h, l = split(w_ref[pl.ds(there, B), q])
                w_ref[rows, q] = w_ref[rows, q] - dot(p, jnp.concatenate([h, l], 0))
                return 0

            return lax.fori_loop(0, N // TILE, tile, 0)

        lax.fori_loop(0, stage, earlier, 0)
    d_ref[...] = w_ref[rows, pl.ds(here, B)]
    block_sweep(d_ref, m_ref, r_ref)
    minus = d_ref[...]
    left = wide(minus)

    def forward(n, _):
        q = pl.ds(pl.multiple_of(n * TILE, TILE), TILE)
        t = -dot(left, tall(w_ref[rows, q]))
        t3_ref[:, q] = tall(t)
        w_ref[rows, q] = t
        return 0

    lax.fori_loop(0, N // TILE, forward, 0)
    w_ref[rows, pl.ds(here, B)] = minus
    if stage:

        def update(j, _):
            back = pl.ds(pl.multiple_of(ids[j] * B, B), B)
            c = wide(w_ref[back, pl.ds(here, B)])
            d_ref[...] = -dot(c, tall(minus))

            def tile(n, _):
                q = pl.ds(pl.multiple_of(n * TILE, TILE), TILE)
                w_ref[back, q] = w_ref[back, q] - dot(c, t3_ref[:, q])
                return 0

            lax.fori_loop(0, N // TILE, tile, 0)
            w_ref[back, pl.ds(here, B)] = d_ref[...]
            return 0

        lax.fori_loop(0, stage, update, 0)
    if stage == N // B - 1:
        c3 = wide(cross_ref[...])

        def gains(j, _):
            q = pl.ds(pl.multiple_of(j * B, B), B)
            g_ref[:, q] = -dot(c3, tall(w_ref[:, q]))
            return 0

        lax.fori_loop(0, N // B, gains, 0)


def sweep_stage(stage, ids, near, far, w, cross):
    last = stage == N // B - 1
    args = [ids, near, far] + ([w] if stage else []) + ([cross] if last else [])
    out = [pltpu.VMEM((N, N), f32)] + ([jax.ShapeDtypeStruct(cross.shape, f32)] if last else [])
    return pl.pallas_call(
        functools.partial(stage_kernel, stage),
        name="stage" + str(stage),
        out_shape=out,
        in_specs=[SMEM_WHOLE] + [VMEM_WHOLE] * (len(args) - 1),
        out_specs=[VMEM_WHOLE] * len(out),
        scratch_shapes=[
            pltpu.VMEM((B, N), bf16),
            pltpu.VMEM((3 * B, N), bf16),
            pltpu.VMEM((B, B), f32),
            pltpu.VMEM((H, H), f32),
            pltpu.VMEM((B, H), f32),
        ],
        input_output_aliases={3: 0} if stage else {},
        compiler_params=pltpu.CompilerParams(vmem_limit_bytes=STAGE_VMEM),
        cost_estimate=pl.CostEstimate(flops=40_000_000_000, bytes_accessed=4 * B * N, transcendentals=0),
    )(*args)


STAGE_VMEM = 24 << 20


def matvec(m_ref, v, out_ref):
    def block(i, _):
        rows = pl.ds(pl.multiple_of(i * LANES, LANES), LANES)
        total = m_ref[rows, :LANES] * v[:, :LANES]
        for j in range(1, N // LANES):
            lanes = slice(j * LANES, (j + 1) * LANES)
            total = total + m_ref[rows, lanes] * v[:, lanes]
        out_ref[:, rows] = jnp.sum(total.T, axis=0, keepdims=True)
        return 0

    lax.fori_loop(0, N // LANES, block, 0)


def turn_kernel(late_ref, base_ref, mean_ref, w_ref, c_ref, s_ref, y_ref):
    matvec(w_ref, late_ref[...] + base_ref[...], y_ref)
    matvec(c_ref, y_ref[...], s_ref)
    s_ref[...] = mean_ref[...] - s_ref[...]


def turn(late, base, mean, minus_inverse, packed):
    return pl.pallas_call(
        turn_kernel,
        out_shape=jax.ShapeDtypeStruct((1, N), f32),
        in_specs=[VMEM_WHOLE] * 5,
        out_specs=VMEM_WHOLE,
        scratch_shapes=[pltpu.VMEM((1, N), f32)],
        compiler_params=pltpu.CompilerParams(vmem_limit_bytes=4 << 20),
        cost_estimate=pl.CostEstimate(flops=4 * N * N, bytes_accessed=8 * N * N, transcendentals=0),
    )(late, base, mean, minus_inverse, packed)


def first_kernel(final_ref, w_ref, x_ref, s_ref, base_ref, mean_ref, y_ref):
    for j in range(N // LANES):
        rows = slice(j * LANES, (j + 1) * LANES)
        vectors = x_ref[rows, N:].T[:8, :]
        mean_ref[:, rows] = vectors[0:1]
        base_ref[:, rows] = jnp.where(final_ref[0] > 0, vectors[2:3], 0.0) - vectors[1:2]
    matvec(w_ref, base_ref[...], y_ref)
    matvec(x_ref, y_ref[...], s_ref)
    s_ref[...] = mean_ref[...] - s_ref[...]


def first_turn(final, minus_inverse, packed):
    return pl.pallas_call(
        first_kernel,
        out_shape=[jax.ShapeDtypeStruct((1, N), f32)] * 3,
        in_specs=[SMEM_WHOLE] + [VMEM_WHOLE] * 2,
        out_specs=[VMEM_WHOLE] * 3,
        scratch_shapes=[pltpu.VMEM((1, N), f32)],
        compiler_params=pltpu.CompilerParams(vmem_limit_bytes=4 << 20),
        cost_estimate=pl.CostEstimate(flops=4 * N * N, bytes_accessed=8 * N * N, transcendentals=0),
    )(final, minus_inverse, packed)


def swap(x, inner):
    pairs = []
    for z in range(Z):
        other = z ^ 1 if inner else (z + (1 if z % 2 else -1)) % Z
        pairs += [(z * Y + y, other * Y + y) for y in range(Y)]
    return lax.ppermute(x, "row", pairs)


def along_y(x, d):
    return lax.ppermute(x, "row", [(z * Y + (y + d) % Y, z * Y + y) for z in range(Z) for y in range(Y)])


def per_device(pred_cov, cross, filt_mean, pred_mean, next_smoothed):
    steps = lax.axis_size("tm")
    row = lax.axis_index("row")
    y, z = row % Y, row // Y
    columns = jnp.stack([filt_mean[0], pred_mean[0], next_smoothed], axis=1)
    packed = jnp.concatenate([cross[0], jnp.pad(columns, ((0, 0), (0, LANES - 3)))], axis=1)
    packed = lax.all_gather(packed, "row", axis=0, tiled=True)

    own = jnp.concatenate([pred_cov[0]] + [along_y(pred_cov[0], d) for d in range(1, Y)], axis=0)
    a1, b1 = swap(own, True), swap(own, False)
    a2, b2 = swap(b1, True), swap(a1, False)
    a3, b3 = swap(b2, True), swap(a2, False)
    b4 = swap(a3, False)
    e = 1 - 2 * (z % 2)
    at = lambda k: (z + e * k + Z) % Z
    order = [at(0) // 2, at(-1) // 2, at(2) // 2, at(-3) // 2]
    ids = lambda m, n: jnp.stack(order + [at(m), at(n), y, y]).astype(jnp.int32)
    w = sweep_stage(0, ids(0, 1), own, a1, None, None)[0]
    w = sweep_stage(1, ids(-1, -2), b1, b2, w, None)[0]
    w = sweep_stage(2, ids(2, 3), a2, a3, w, None)[0]
    minus_inverse, gain = sweep_stage(3, ids(-3, -4), b3, b4, w, cross[0])

    final = lax.axis_index("tm") == steps - 1
    state, base, mean = first_turn(final.astype(f32)[None], minus_inverse, packed)
    for _ in range(steps - 1):
        late = lax.ppermute(state, "tm", [(i, i - 1) for i in range(1, steps)])
        state = turn(late, base, mean, minus_inverse, packed)
    smoothed = lax.dynamic_slice(state[0], (row * MINE,), (MINE,))
    return (smoothed[None, :], gain[None, :, :])


def solution(mesh):
    in_specs = (
        P("tm", "row", None),
        P("tm", "row", None),
        P("tm", "row"),
        P("tm", "row"),
        P("row"),
    )
    out_specs = (P("tm", "row"), P("tm", "row", None))
    return jax.shard_map(
        per_device, mesh=mesh, in_specs=in_specs, out_specs=out_specs, check_vma=False
    )
```

time: 302 us -> 265 us (0.88)
  waiting for transfers between devices: 106 us -> 45 us
  starting transfers between devices: 17.3 us -> 40.3 us
  Pallas kernels: 135 us -> 142 us
  local copies, waits for them, and re-layouts: 26.4 us -> 19.8 us
    all_gather x1 -> x0, waiting for transfers between devices: 84.8 us -> none  [per_device(): whole_cov = lax.all_gather(pred_cov[0], 'row', axis=0, tiled=True)]
    ppermute x0 -> x10, starting transfers between devices: none -> 24.6 us  [the longest x7 19.9 us: swap(): return lax.ppermute(x, 'row', pairs)]
    ppermute x0 -> x10, waiting for transfers between devices: none -> 24.5 us  [the longest x7 14.9 us: swap(): return lax.ppermute(x, 'row', pairs)]
    pallas_call x8 -> x7, Pallas kernels: 10.5 us -> 22.4 us  [turn(): pl.pallas_call(turn_kernel, out_shape=jax.ShapeDtypeStruct((1, N), f32),...]
    unnamed x16 -> x14, local copies, waits for them, and re-layouts: 25.7 us -> 18.8 us
    pallas_call x2 -> x5, Pallas kernels: 124 us -> 119 us  [the longest x4 116 us: sweep_stage(): pl.pallas_call(functools.partial(stage_kernel, stage), name='stage' + str...]
  transfers between devices with their start and end apart: 9 -> 18, of which waited for: 8 -> 11; matrix products, arithmetic and copies ran while one was open for 1% -> 0% of each run, Pallas kernels for 41% -> 44%
where the time goes in v2:
time: 265 us; the launch traced here: 264 us
  Pallas kernels  142 us (54%)
  waiting for transfers between devices  45 us (17%)
  starting transfers between devices  40.3 us (15%)
  local copies, waits for them, and re-layouts  19.8 us (7%)
  between operations  14.2 us (5%)
  other arithmetic  3.35 us (1%)
    pallas_call x4, Pallas kernels, sweep_stage(): pl.pallas_call(functools.partial(stage_kernel, stage), name='stage' + str...  116 us
    pallas_call x7, Pallas kernels, turn(): pl.pallas_call(turn_kernel, out_shape=jax.ShapeDtypeStruct((1, N), f32),...  22.4 us
    ppermute x7, waiting for transfers between devices, per_device(): late = lax.ppermute(state, 'tm', [(i, i - 1) for i in range(1, steps)])  20.5 us
    ppermute x7, starting transfers between devices, swap(): return lax.ppermute(x, 'row', pairs)  19.9 us
    unnamed x14, local copies, waits for them, and re-layouts  18.8 us
    ppermute x7, starting transfers between devices, per_device(): late = lax.ppermute(state, 'tm', [(i, i - 1) for i in range(1, steps)])  15.7 us
    ppermute x7, waiting for transfers between devices, swap(): return lax.ppermute(x, 'row', pairs)  14.9 us
    ppermute x3, waiting for transfers between devices, along_y(): lax.ppermute(x, 'row', [(z * Y + (y + d) % Y, z * Y + y) for z in range(Z...  9.6 us
  transfers between devices with their start and end apart: 18, of which 11 were waited for; matrix products, arithmetic and copies ran while one was open for 0% of the time, Pallas kernels for 44%

profile of v2, /device:TPU:1, one launch (start us, length us, event | category | flops | bytes accessed | tf_op | source)
XLA Modules:
  0.0 264.4 jit_solution(11367659710285510968)
XLA Ops:
  9.7 3.6 %collective-permute-start = (bf16[48,1536]{1,0:T(8,128)(2,1)}, bf16[48,1536]{1,0:T(8,128)(2,1)S(1)}, u32[]{:S(2)}, u32[]{:S(2)}) collective-permute-start(bf16[48,1536]{1,0:T(8,128)(2,1)} %bitcast.22), channel_id=1, source_target_pairs={{1,0},{2,1},{3,2},{0,3},{5,4},{6,5},{7,6},{4,7},{9,8},{10,9},{11,1... | collective-permute-start | bytes 442376 | tf_op jit(solution)/shard_map/ppermute | solution.py:269
  14.4 3.5 %collective-permute-done = bf16[48,1536]{1,0:T(8,128)(2,1)S(1)} collective-permute-done((bf16[48,1536]{1,0:T(8,128)(2,1)}, bf16[48,1536]{1,0:T(8,128)(2,1)S(1)}, u32[]{:S(2)}, u32[]{:S(2)}) %collective-permute-start) | collective-permute-done | bytes 147488 | tf_op jit(solution)/shard_map/ppermute | solution.py:269
  19.5 4.5 %collective-permute-done.2 = bf16[48,1536]{1,0:T(8,128)(2,1)S(1)} collective-permute-done((bf16[48,1536]{1,0:T(8,128)(2,1)}, bf16[48,1536]{1,0:T(8,128)(2,1)S(1)}, u32[]{:S(2)}, u32[]{:S(2)}) %collective-permute-start.2) | collective-permute-done | bytes 147488 | tf_op jit(solution)/shard_map/ppermute | solution.py:269
  26.7 4.7 %collective-permute-start.3 = (bf16[192,1536]{1,0:T(8,128)(2,1)S(1)}, bf16[192,1536]{1,0:T(8,128)(2,1)S(1)}, u32[]{:S(2)}, u32[]{:S(2)}) collective-permute-start(bf16[192,1536]{1,0:T(8,128)(2,1)S(1)} %pad_maximum_fusion.near_ref), channel_id=1, source_target_pairs={{0,28},{1,29},{2,30},{3,31},{4,8},{5,9},{6,10},{7,11},{8,4},{9,5},... | collective-permute-start | bytes 1769480 | tf_op jit(solution)/shard_map/ppermute | solution.py:265
  31.7 14.9 %collective-permute-done.6.far_ref = bf16[192,1536]{1,0:T(8,128)(2,1)S(1)} collective-permute-done((bf16[192,1536]{1,0:T(8,128)(2,1)S(1)}, bf16[192,1536]{1,0:T(8,128)(2,1)S(1)}, u32[]{:S(2)}, u32[]{:S(2)}) %collective-permute-start.6) | collective-permute-done | bytes 589856 | tf_op jit(solution)/shard_map/ppermute | solution.py:265
  46.6 9.2 %collective-permute-start.7 = (bf16[192,1536]{1,0:T(8,128)(2,1)S(1)}, bf16[192,1536]{1,0:T(8,128)(2,1)S(1)}, u32[]{:S(2)}, u32[]{:S(2)}) collective-permute-start(bf16[192,1536]{1,0:T(8,128)(2,1)S(1)} %collective-permute-done.6.far_ref), channel_id=1, source_target_pairs={{0,28},{1,29},{2,30},{3,31},{4,8},{5,9},{6,10},{7,11},{8,4},{9,5},... | collective-permute-start | bytes 1769480 | tf_op jit(solution)/shard_map/ppermute | solution.py:265
  55.8 21.4 %stage0.1.refs_0_ = f32[1536,1536]{1,0:T(8,128)S(1)} custom-call(s32[8]{0:T(128)S(1)} %stack.92.ids, bf16[192,1536]{1,0:T(8,128)(2,1)S(1)} %pad_maximum_fusion.near_ref, bf16[192,1536]{1,0:T(8,128)(2,1)S(1)} %collective-permute-done.6.far_ref), custom_call_target="tpu_custom_call" | custom-call | flops 40000000000 | bytes 2359296 | tf_op jit(solution)/shard_map/stage0/pallas_call | solution.py:184
  79.3 25.7 %stage1.1.refs_0_ = f32[1536,1536]{1,0:T(8,128)S(1)} custom-call(s32[8]{0:T(128)S(1)} %stack.89.ids, bf16[192,1536]{1,0:T(8,128)(2,1)S(1)} %collective-permute-done.3.near_ref, bf16[192,1536]{1,0:T(8,128)(2,1)S(1)} %collective-permute-done.7.far_ref, f32[1536,1536]{1,0:T(8,128)S(1)} %stage0.1.refs_0_), custom_call_target="tpu_custom_call", output_to_operand_aliasing={{}: (3, {})} | custom-call | flops 40000000000 | bytes 2359296 | tf_op jit(solution)/shard_map/stage1/pallas_call | solution.py:184
  105.1 2.3 collective-permute-start.9
  107.4 30.3 %stage2.1.refs_0_ = f32[1536,1536]{1,0:T(8,128)S(1)} custom-call(s32[8]{0:T(128)S(1)} %stack.86.ids, bf16[192,1536]{1,0:T(8,128)(2,1)S(1)} %collective-permute-done.4.near_ref, bf16[192,1536]{1,0:T(8,128)(2,1)S(1)} %collective-permute-done.8.far_ref, f32[1536,1536]{1,0:T(8,128)S(1)} %stage1.1.refs_0_), custom_call_target="tpu_custom_call", output_to_operand_aliasing={{}: (3, {})} | custom-call | flops 40000000000 | bytes 2359296 | tf_op jit(solution)/shard_map/stage2/pallas_call | solution.py:184
  137.7 38.4 %stage3.1 = (f32[1536,1536]{1,0:T(8,128)S(1)}, f32[48,1536]{1,0:T(8,128)}) custom-call(s32[8]{0:T(128)S(1)} %stack.83.ids, bf16[192,1536]{1,0:T(8,128)(2,1)S(1)} %collective-permute-done.5.near_ref, bf16[192,1536]{1,0:T(8,128)(2,1)S(1)} %collective-permute-done.9.far_ref, f32[1536,1536]{1,0:T(8,128)S(1)} %stage2.1.refs_0_, ...), custom_call_target="tpu_custom_call", output_to_operand_aliasing={{0}: (3, {})} | custom-call | flops 40000000000 | bytes 2359296 | tf_op jit(solution)/shard_map/stage3/pallas_call | solution.py:184
  176.1 3.6 %copy-done.3 = f32[1536,1536]{1,0:T(8,128)} copy-done((f32[1536,1536]{1,0:T(8,128)}, f32[1536,1536]{1,0:T(8,128)S(1)}, u32[]{:S(2)}) %copy-start.3) | copy-done | bytes 9437208
  179.7 3.9 %copy-done = f32[1536,1664]{1,0:T(8,128)S(1)} copy-done((f32[1536,1664]{1,0:T(8,128)S(1)}, f32[1536,1664]{1,0:T(8,128)}, u32[]{:S(2)}) %copy-start) | copy-done | bytes 10223640
  183.6 3.7 %copy-done.4 = f32[1536,1536]{1,0:T(8,128)S(1)} copy-done((f32[1536,1536]{1,0:T(8,128)S(1)}, f32[1536,1536]{1,0:T(8,128)}, u32[]{:S(2)}) %copy-start.4) | copy-done | bytes 9437208
  187.3 3.5 %shard_map.68 = (f32[1,1536]{1,0:T(1,128)S(1)}, f32[1,1536]{1,0:T(1,128)S(1)}, f32[1,1536]{1,0:T(1,128)S(1)}) custom-call(f32[1]{0:T(128)} %bitcast.final_ref, f32[1536,1536]{1,0:T(8,128)S(1)} %copy-done.4, f32[1536,1664]{1,0:T(8,128)S(1)} %copy-done), custom_call_target="tpu_custom_call" | custom-call | flops 9437184 | bytes 18874368 | tf_op jit(solution)/shard_map/pallas_call | solution.py:249
  190.7 4.2 %collective-permute-start.10 = (f32[1,1536]{1,0:T(1,128)S(1)}, f32[1,1536]{1,0:T(1,128)S(1)}, u32[]{:S(2)}, u32[]{:S(2)}) collective-permute-start(f32[1,1536]{1,0:T(1,128)S(1)} %get-tuple-element.8), channel_id=1, source_target_pairs={{32,0},{64,32},{96,64},{128,96},{160,128},{192,160},{224,192},{33,... | collective-permute-start | bytes 18440 | tf_op jit(solution)/shard_map/ppermute | solution.py:297
  194.9 2.4 collective-permute-done.10.late_ref
  197.3 3.2 %shard_map.69 = f32[1,1536]{1,0:T(1,128)S(1)} custom-call(f32[1,1536]{1,0:T(1,128)S(1)} %collective-permute-done.10.late_ref, f32[1,1536]{1,0:T(1,128)S(1)} %get-tuple-element.9.base_ref, f32[1,1536]{1,0:T(1,128)S(1)} %get-tuple-element.10.mean_ref, f32[1536,1536]{1,0:T(8,128)S(1)} %copy-done.4, f32[1536,1664]{1,0:T(8,128)S(1)} %copy-done.1), custom_call_target="tpu_custom_call" | custom-call | flops 9437184 | bytes 18874368 | tf_op jit(solution)/shard_map/pallas_call | solution.py:226
  202.4 3.0 %collective-permute-done.11.late_ref = f32[1,1536]{1,0:T(1,128)S(1)} collective-permute-done((f32[1,1536]{1,0:T(1,128)S(1)}, f32[1,1536]{1,0:T(1,128)S(1)}, u32[]{:S(2)}, u32[]{:S(2)}) %collective-permute-start.11) | collective-permute-done | bytes 6176 | tf_op jit(solution)/shard_map/ppermute | solution.py:297
  205.4 3.2 %shard_map.70 = f32[1,1536]{1,0:T(1,128)S(1)} custom-call(f32[1,1536]{1,0:T(1,128)S(1)} %collective-permute-done.11.late_ref, f32[1,1536]{1,0:T(1,128)S(1)} %get-tuple-element.9.base_ref, f32[1,1536]{1,0:T(1,128)S(1)} %get-tuple-element.10.mean_ref, f32[1536,1536]{1,0:T(8,128)S(1)} %copy-done.4, f32[1536,1664]{1,0:T(8,128)S(1)} %copy-done.1), custom_call_target="tpu_custom_call" | custom-call | flops 9437184 | bytes 18874368 | tf_op jit(solution)/shard_map/pallas_call | solution.py:226
  210.6 3.0 %collective-permute-done.12.late_ref = f32[1,1536]{1,0:T(1,128)S(1)} collective-permute-done((f32[1,1536]{1,0:T(1,128)S(1)}, f32[1,1536]{1,0:T(1,128)S(1)}, u32[]{:S(2)}, u32[]{:S(2)}) %collective-permute-start.12) | collective-permute-done | bytes 6176 | tf_op jit(solution)/shard_map/ppermute | solution.py:297
  213.6 3.2 %shard_map.71 = f32[1,1536]{1,0:T(1,128)S(1)} custom-call(f32[1,1536]{1,0:T(1,128)S(1)} %collective-permute-done.12.late_ref, f32[1,1536]{1,0:T(1,128)S(1)} %get-tuple-element.9.base_ref, f32[1,1536]{1,0:T(1,128)S(1)} %get-tuple-element.10.mean_ref, f32[1536,1536]{1,0:T(8,128)S(1)} %copy-done.4, f32[1536,1664]{1,0:T(8,128)S(1)} %copy-done.1), custom_call_target="tpu_custom_call" | custom-call | flops 9437184 | bytes 18874368 | tf_op jit(solution)/shard_map/pallas_call | solution.py:226
  218.7 3.0 %collective-permute-done.13.late_ref = f32[1,1536]{1,0:T(1,128)S(1)} collective-permute-done((f32[1,1536]{1,0:T(1,128)S(1)}, f32[1,1536]{1,0:T(1,128)S(1)}, u32[]{:S(2)}, u32[]{:S(2)}) %collective-permute-start.13) | collective-permute-done | bytes 6176 | tf_op jit(solution)/shard_map/ppermute | solution.py:297
  221.8 3.2 %shard_map.72 = f32[1,1536]{1,0:T(1,128)S(1)} custom-call(f32[1,1536]{1,0:T(1,128)S(1)} %collective-permute-done.13.late_ref, f32[1,1536]{1,0:T(1,128)S(1)} %get-tuple-element.9.base_ref, f32[1,1536]{1,0:T(1,128)S(1)} %get-tuple-element.10.mean_ref, f32[1536,1536]{1,0:T(8,128)S(1)} %copy-done.4, f32[1536,1664]{1,0:T(8,128)S(1)} %copy-done.1), custom_call_target="tpu_custom_call" | custom-call | flops 9437184 | bytes 18874368 | tf_op jit(solution)/shard_map/pallas_call | solution.py:226
  226.9 3.0 %collective-permute-done.14.late_ref = f32[1,1536]{1,0:T(1,128)S(1)} collective-permute-done((f32[1,1536]{1,0:T(1,128)S(1)}, f32[1,1536]{1,0:T(1,128)S(1)}, u32[]{:S(2)}, u32[]{:S(2)}) %collective-permute-start.14) | collective-permute-done | bytes 6176 | tf_op jit(solution)/shard_map/ppermute | solution.py:297
  229.9 3.2 %shard_map.73 = f32[1,1536]{1,0:T(1,128)S(1)} custom-call(f32[1,1536]{1,0:T(1,128)S(1)} %collective-permute-done.14.late_ref, f32[1,1536]{1,0:T(1,128)S(1)} %get-tuple-element.9.base_ref, f32[1,1536]{1,0:T(1,128)S(1)} %get-tuple-element.10.mean_ref, f32[1536,1536]{1,0:T(8,128)S(1)} %copy-done.4, f32[1536,1664]{1,0:T(8,128)S(1)} %copy-done.1), custom_call_target="tpu_custom_call" | custom-call | flops 9437184 | bytes 18874368 | tf_op jit(solution)/shard_map/pallas_call | solution.py:226
  235.0 3.0 %collective-permute-done.15.late_ref = f32[1,1536]{1,0:T(1,128)S(1)} collective-permute-done((f32[1,1536]{1,0:T(1,128)S(1)}, f32[1,1536]{1,0:T(1,128)S(1)}, u32[]{:S(2)}, u32[]{:S(2)}) %collective-permute-start.15) | collective-permute-done | bytes 6176 | tf_op jit(solution)/shard_map/ppermute | solution.py:297
  238.1 3.2 %shard_map.74 = f32[1,1536]{1,0:T(1,128)S(1)} custom-call(f32[1,1536]{1,0:T(1,128)S(1)} %collective-permute-done.15.late_ref, f32[1,1536]{1,0:T(1,128)S(1)} %get-tuple-element.9.base_ref, f32[1,1536]{1,0:T(1,128)S(1)} %get-tuple-element.10.mean_ref, f32[1536,1536]{1,0:T(8,128)S(1)} %copy-done.4, f32[1536,1664]{1,0:T(8,128)S(1)} %copy-done.1), custom_call_target="tpu_custom_call" | custom-call | flops 9437184 | bytes 18874368 | tf_op jit(solution)/shard_map/pallas_call | solution.py:226
  243.2 3.0 %collective-permute-done.16.late_ref = f32[1,1536]{1,0:T(1,128)S(1)} collective-permute-done((f32[1,1536]{1,0:T(1,128)S(1)}, f32[1,1536]{1,0:T(1,128)S(1)}, u32[]{:S(2)}, u32[]{:S(2)}) %collective-permute-start.16) | collective-permute-done | bytes 6176 | tf_op jit(solution)/shard_map/ppermute | solution.py:297
  246.2 3.9 %copy-done.2 = f32[1536,1664]{1,0:T(8,128)S(1)} copy-done((f32[1536,1664]{1,0:T(8,128)S(1)}, f32[1536,1664]{1,0:T(8,128)}, u32[]{:S(2)}) %copy-start.2) | copy-done | bytes 10223640
  250.1 3.7 %copy-done.5 = f32[1536,1536]{1,0:T(8,128)S(1)} copy-done((f32[1536,1536]{1,0:T(8,128)S(1)}, f32[1536,1536]{1,0:T(8,128)}, u32[]{:S(2)}) %copy-start.5) | copy-done | bytes 9437208
  253.8 3.2 %shard_map.75 = f32[1,1536]{1,0:T(1,128)S(1)} custom-call(f32[1,1536]{1,0:T(1,128)S(1)} %collective-permute-done.16.late_ref, f32[1,1536]{1,0:T(1,128)S(1)} %get-tuple-element.9.base_ref, f32[1,1536]{1,0:T(1,128)S(1)} %get-tuple-element.10.mean_ref, f32[1536,1536]{1,0:T(8,128)S(1)} %copy-done.5, f32[1536,1664]{1,0:T(8,128)S(1)} %copy-done.2), custom_call_target="tpu_custom_call" | custom-call | flops 9437184 | bytes 18874368 | tf_op jit(solution)/shard_map/pallas_call | solution.py:226
  (40 shorter events, 22.4 us)
Async XLA Ops:
  7.2 172.5 %all-gather.2.cloned.1.call-start = ((), (), s32[]{:S(2)}) async-start(), calls=%async_computation | async-start | bytes 10543104 | tf_op jit(solution)/shard_map/all_gather | solution.py:278
  9.7 8.2 %collective-permute-start = (bf16[48,1536]{1,0:T(8,128)(2,1)}, bf16[48,1536]{1,0:T(8,128)(2,1)S(1)}, u32[]{:S(2)}, u32[]{:S(2)}) collective-permute-start(bf16[48,1536]{1,0:T(8,128)(2,1)} %bitcast.22), channel_id=1, source_target_pairs={{1,0},{2,1},{3,2},{0,3},{5,4},{6,5},{7,6},{4,7},{9,8},{10,9},{11,1... | collective-permute-start | bytes 442376 | tf_op jit(solution)/shard_map/ppermute | solution.py:269
  13.4 6.1 %collective-permute-start.1 = (bf16[48,1536]{1,0:T(8,128)(2,1)}, bf16[48,1536]{1,0:T(8,128)(2,1)S(1)}, u32[]{:S(2)}, u32[]{:S(2)}) collective-permute-start(bf16[48,1536]{1,0:T(8,128)(2,1)} %bitcast.23), channel_id=1, source_target_pairs={{2,0},{3,1},{0,2},{1,3},{6,4},{7,5},{4,6},{5,7},{10,8},{11,9},{8,1... | collective-permute-start | bytes 442376 | tf_op jit(solution)/shard_map/ppermute | solution.py:269
  13.7 10.3 %collective-permute-start.2 = (bf16[48,1536]{1,0:T(8,128)(2,1)}, bf16[48,1536]{1,0:T(8,128)(2,1)S(1)}, u32[]{:S(2)}, u32[]{:S(2)}) collective-permute-start(bf16[48,1536]{1,0:T(8,128)(2,1)} %bitcast.24), channel_id=1, source_target_pairs={{3,0},{0,1},{1,2},{2,3},{7,4},{4,5},{5,6},{6,7},{11,8},{8,9},{9,10... | collective-permute-start | bytes 442376 | tf_op jit(solution)/shard_map/ppermute | solution.py:269
  25.0 21.6 %collective-permute-start.6 = (bf16[192,1536]{1,0:T(8,128)(2,1)S(1)}, bf16[192,1536]{1,0:T(8,128)(2,1)S(1)}, u32[]{:S(2)}, u32[]{:S(2)}) collective-permute-start(bf16[192,1536]{1,0:T(8,128)(2,1)S(1)} %pad_maximum_fusion.near_ref), channel_id=1, source_target_pairs={{0,4},{1,5},{2,6},{3,7},{4,0},{5,1},{6,2},{7,3},{8,12},{9,13},{10,... | collective-permute-start | bytes 1769480 | tf_op jit(solution)/shard_map/ppermute | solution.py:265
  26.7 29.1 %collective-permute-start.3 = (bf16[192,1536]{1,0:T(8,128)(2,1)S(1)}, bf16[192,1536]{1,0:T(8,128)(2,1)S(1)}, u32[]{:S(2)}, u32[]{:S(2)}) collective-permute-start(bf16[192,1536]{1,0:T(8,128)(2,1)S(1)} %pad_maximum_fusion.near_ref), channel_id=1, source_target_pairs={{0,28},{1,29},{2,30},{3,31},{4,8},{5,9},{6,10},{7,11},{8,4},{9,5},... | collective-permute-start | bytes 1769480 | tf_op jit(solution)/shard_map/ppermute | solution.py:265
  46.6 30.7 %collective-permute-start.7 = (bf16[192,1536]{1,0:T(8,128)(2,1)S(1)}, bf16[192,1536]{1,0:T(8,128)(2,1)S(1)}, u32[]{:S(2)}, u32[]{:S(2)}) collective-permute-start(bf16[192,1536]{1,0:T(8,128)(2,1)S(1)} %collective-permute-done.6.far_ref), channel_id=1, source_target_pairs={{0,28},{1,29},{2,30},{3,31},{4,8},{5,9},{6,10},{7,11},{8,4},{9,5},... | collective-permute-start | bytes 1769480 | tf_op jit(solution)/shard_map/ppermute | solution.py:265
  55.8 23.0 %collective-permute-start.4 = (bf16[192,1536]{1,0:T(8,128)(2,1)S(1)}, bf16[192,1536]{1,0:T(8,128)(2,1)S(1)}, u32[]{:S(2)}, u32[]{:S(2)}) collective-permute-start(bf16[192,1536]{1,0:T(8,128)(2,1)S(1)} %collective-permute-done.3.near_ref), channel_id=1, source_target_pairs={{0,4},{1,5},{2,6},{3,7},{4,0},{5,1},{6,2},{7,3},{8,12},{9,13},{10,... | collective-permute-start | bytes 1769480 | tf_op jit(solution)/shard_map/ppermute | solution.py:265
  77.3 27.8 %collective-permute-start.8 = (bf16[192,1536]{1,0:T(8,128)(2,1)S(1)}, bf16[192,1536]{1,0:T(8,128)(2,1)S(1)}, u32[]{:S(2)}, u32[]{:S(2)}) collective-permute-start(bf16[192,1536]{1,0:T(8,128)(2,1)S(1)} %collective-permute-done.7.far_ref), channel_id=1, source_target_pairs={{0,4},{1,5},{2,6},{3,7},{4,0},{5,1},{6,2},{7,3},{8,12},{9,13},{10,... | collective-permute-start | bytes 1769480 | tf_op jit(solution)/shard_map/ppermute | solution.py:265
  78.8 58.8 %collective-permute-start.5 = (bf16[192,1536]{1,0:T(8,128)(2,1)S(1)}, bf16[192,1536]{1,0:T(8,128)(2,1)S(1)}, u32[]{:S(2)}, u32[]{:S(2)}) collective-permute-start(bf16[192,1536]{1,0:T(8,128)(2,1)S(1)} %collective-permute-done.4.near_ref), channel_id=1, source_target_pairs={{0,28},{1,29},{2,30},{3,31},{4,8},{5,9},{6,10},{7,11},{8,4},{9,5},... | collective-permute-start | bytes 1769480 | tf_op jit(solution)/shard_map/ppermute | solution.py:265
  105.1 32.6 %copy-start.6 = (f32[1,48,1536]{2,1,0:T(8,128)S(1)}, f32[1,48,1536]{2,1,0:T(8,128)}, u32[]{:S(2)}) copy-start(f32[1,48,1536]{2,1,0:T(8,128)} %param.6) | copy-start | bytes 884740
  105.1 32.5 %collective-permute-start.9 = (bf16[192,1536]{1,0:T(8,128)(2,1)S(1)}, bf16[192,1536]{1,0:T(8,128)(2,1)S(1)}, u32[]{:S(2)}, u32[]{:S(2)}) collective-permute-start(bf16[192,1536]{1,0:T(8,128)(2,1)S(1)} %collective-permute-done.8.far_ref), channel_id=1, source_target_pairs={{0,28},{1,29},{2,30},{3,31},{4,8},{5,9},{6,10},{7,11},{8,4},{9,5},... | collective-permute-start | bytes 1769480 | tf_op jit(solution)/shard_map/ppermute | solution.py:265
  176.1 3.6 %copy-start.3 = (f32[1536,1536]{1,0:T(8,128)}, f32[1536,1536]{1,0:T(8,128)S(1)}, u32[]{:S(2)}) copy-start(f32[1536,1536]{1,0:T(8,128)S(1)} %get-tuple-element.7.w_ref) | copy-start | bytes 28311556
  179.7 3.9 %copy-start = (f32[1536,1664]{1,0:T(8,128)S(1)}, f32[1536,1664]{1,0:T(8,128)}, u32[]{:S(2)}) copy-start(f32[1536,1664]{1,0:T(8,128)} %all-gather.2.cloned.1.call-done.x_ref.c_ref) | copy-start | bytes 30670852
  183.6 3.7 %copy-start.4 = (f32[1536,1536]{1,0:T(8,128)S(1)}, f32[1536,1536]{1,0:T(8,128)}, u32[]{:S(2)}) copy-start(f32[1536,1536]{1,0:T(8,128)} %copy-done.3) | copy-start | bytes 28311556
  187.3 10.0 %copy-start.1 = (f32[1536,1664]{1,0:T(8,128)S(1)}, f32[1536,1664]{1,0:T(8,128)}, u32[]{:S(2)}) copy-start(f32[1536,1664]{1,0:T(8,128)} %all-gather.2.cloned.1.call-done.x_ref.c_ref) | copy-start | bytes 30670852
  190.7 6.6 %collective-permute-start.10 = (f32[1,1536]{1,0:T(1,128)S(1)}, f32[1,1536]{1,0:T(1,128)S(1)}, u32[]{:S(2)}, u32[]{:S(2)}) collective-permute-start(f32[1,1536]{1,0:T(1,128)S(1)} %get-tuple-element.8), channel_id=1, source_target_pairs={{32,0},{64,32},{96,64},{128,96},{160,128},{192,160},{224,192},{33,... | collective-permute-start | bytes 18440 | tf_op jit(solution)/shard_map/ppermute | solution.py:297
  200.5 4.9 %collective-permute-start.11 = (f32[1,1536]{1,0:T(1,128)S(1)}, f32[1,1536]{1,0:T(1,128)S(1)}, u32[]{:S(2)}, u32[]{:S(2)}) collective-permute-start(f32[1,1536]{1,0:T(1,128)S(1)} %shard_map.69), channel_id=1, source_target_pairs={{32,0},{64,32},{96,64},{128,96},{160,128},{192,160},{224,192},{33,... | collective-permute-start | bytes 18440 | tf_op jit(solution)/shard_map/ppermute | solution.py:297
  208.7 4.9 %collective-permute-start.12 = (f32[1,1536]{1,0:T(1,128)S(1)}, f32[1,1536]{1,0:T(1,128)S(1)}, u32[]{:S(2)}, u32[]{:S(2)}) collective-permute-start(f32[1,1536]{1,0:T(1,128)S(1)} %shard_map.70), channel_id=1, source_target_pairs={{32,0},{64,32},{96,64},{128,96},{160,128},{192,160},{224,192},{33,... | collective-permute-start | bytes 18440 | tf_op jit(solution)/shard_map/ppermute | solution.py:297
  216.8 4.9 %collective-permute-start.13 = (f32[1,1536]{1,0:T(1,128)S(1)}, f32[1,1536]{1,0:T(1,128)S(1)}, u32[]{:S(2)}, u32[]{:S(2)}) collective-permute-start(f32[1,1536]{1,0:T(1,128)S(1)} %shard_map.71), channel_id=1, source_target_pairs={{32,0},{64,32},{96,64},{128,96},{160,128},{192,160},{224,192},{33,... | collective-permute-start | bytes 18440 | tf_op jit(solution)/shard_map/ppermute | solution.py:297
  225.0 4.9 %collective-permute-start.14 = (f32[1,1536]{1,0:T(1,128)S(1)}, f32[1,1536]{1,0:T(1,128)S(1)}, u32[]{:S(2)}, u32[]{:S(2)}) collective-permute-start(f32[1,1536]{1,0:T(1,128)S(1)} %shard_map.72), channel_id=1, source_target_pairs={{32,0},{64,32},{96,64},{128,96},{160,128},{192,160},{224,192},{33,... | collective-permute-start | bytes 18440 | tf_op jit(solution)/shard_map/ppermute | solution.py:297
  233.1 4.9 %collective-permute-start.15 = (f32[1,1536]{1,0:T(1,128)S(1)}, f32[1,1536]{1,0:T(1,128)S(1)}, u32[]{:S(2)}, u32[]{:S(2)}) collective-permute-start(f32[1,1536]{1,0:T(1,128)S(1)} %shard_map.73), channel_id=1, source_target_pairs={{32,0},{64,32},{96,64},{128,96},{160,128},{192,160},{224,192},{33,... | collective-permute-start | bytes 18440 | tf_op jit(solution)/shard_map/ppermute | solution.py:297
  241.3 4.9 %collective-permute-start.16 = (f32[1,1536]{1,0:T(1,128)S(1)}, f32[1,1536]{1,0:T(1,128)S(1)}, u32[]{:S(2)}, u32[]{:S(2)}) collective-permute-start(f32[1,1536]{1,0:T(1,128)S(1)} %shard_map.74), channel_id=1, source_target_pairs={{32,0},{64,32},{96,64},{128,96},{160,128},{192,160},{224,192},{33,... | collective-permute-start | bytes 18440 | tf_op jit(solution)/shard_map/ppermute | solution.py:297
  246.2 3.9 %copy-start.2 = (f32[1536,1664]{1,0:T(8,128)S(1)}, f32[1536,1664]{1,0:T(8,128)}, u32[]{:S(2)}) copy-start(f32[1536,1664]{1,0:T(8,128)} %all-gather.2.cloned.1.call-done.x_ref.c_ref) | copy-start | bytes 30670852
  250.1 3.7 %copy-start.5 = (f32[1536,1536]{1,0:T(8,128)S(1)}, f32[1536,1536]{1,0:T(8,128)}, u32[]{:S(2)}) copy-start(f32[1536,1536]{1,0:T(8,128)} %copy-done.3) | copy-start | bytes 28311556
Sparse Core Ops, SparseCore 0:
  10.6 136.1 all-gather.1
